TPU v7x, 256 devices: a whole 4x4x8 slice. The times are simulated.
256 devices in a mesh: proj: 16 (over x, y_lo, core), tile: 16 (over z, y_hi).
Axes of the slice: x: 4, y: 4 (y_hi: 2, y_lo: 2; y = y_hi * 2 + y_lo), z: 8, core: 2. Of those that a mesh axis runs over, the one named last changes fastest.
Arguments:
- raw: bfloat16 [32, 1024, 4096], P(None, 'proj', 'tile'), may hold values from -6 to 6
- row_weights: bfloat16 [32, 16, 128, 256], P('proj', 'tile'), may hold values from 0 to 1
- col_weights: bfloat16 [32, 16, 1024, 2048], P('proj', 'tile'), may hold values from 0 to 1
- band_start: int32 [32, 16], replicated, may hold values from 0 to 768
- band_length: int32 [32, 16], replicated, may hold values from 64 to 256, as said below
- col_offset: int32 [32, 16], P('proj', 'tile'), may hold values from 0 to 24
Outputs:
- slab: float32 [128, 32768], P('proj', 'tile')
Inputs may be any that keep to these rules, and one draw needn't show every extreme that they name: `band_length`: in every projection some tile uses exactly 256 rows.
All inputs are finite; a program needn't handle non-finite values.
Results may differ from a plain program's by a relative error of at most 0.008.
Values may be sent and summed in bfloat16 or wider, within the bound.
No kernel may reach another device: no remote copies, remote signals or barrier semaphores. Data moves between devices by JAX's collectives and lax.ppermute only.
A program may use at most 128 MiB of HBM per device.

v0:
```python
import math
import jax
import jax.numpy as jnp
from jax import lax
from jax.sharding import PartitionSpec as P

LMAX = 256


def with_halo(array, sides, width):
    for axis, dim in sides:
        count, length = (lax.axis_size(axis), array.shape[dim])
        up = [(i, (i + 1) % count) for i in range(count - 1)]
        down = [(j, i) for i, j in up]
        last = lax.slice_in_dim(array, length - width, length, axis=dim)
        leading = lax.slice_in_dim(array, 0, width, axis=dim)
        before = lax.ppermute(last, axis, up)
        after = lax.ppermute(leading, axis, down)
        array = jnp.concatenate([before, array, after], axis=dim)
    return array


def tap_tiles():
    rows_a = jnp.arange(128, dtype=jnp.int32)[:, None]
    cols_c = jnp.arange(128, dtype=jnp.int32)[None, :]
    tiles = []
    for shift in (-1, 0, 1):
        offset = cols_c - rows_a - 128 * shift
        offset_f = offset.astype(jnp.float32)
        odd_mask = offset % 2 != 0
        safe_sq = jnp.where(offset == 0, 1.0, offset_f * offset_f)
        value = jnp.where(
            offset == 0, 0.25, jnp.where(odd_mask, -1.0 / (math.pi * math.pi * safe_sq), 0.0)
        )
        value = jnp.where((offset >= -128) & (offset <= 127), value, 0.0)
        tiles.append(value.astype(jnp.bfloat16))
    return tiles


def mask_rows(rows, length):
    mask = jnp.arange(rows.shape[0], dtype=jnp.int32)[:, None] < length
    return jnp.where(mask, rows, jnp.zeros_like(rows))


def take_band(proj_data, start, length):
    return mask_rows(lax.dynamic_slice_in_dim(proj_data, start, LMAX, 0), length)


def body(raw, row_weights, col_weights, band_start, band_length, col_offset):
    proj_count, rows_dev, cols_dev = raw.shape
    n_proj = lax.axis_size("proj")
    n_tile = lax.axis_size("tile")
    proj_me = lax.axis_index("proj")
    tile_me = lax.axis_index("tile")
    total_rows = rows_dev * n_proj
    total_cols = cols_dev * n_tile
    dist = 2.0 * total_cols
    row_ids = (proj_me * rows_dev + jnp.arange(rows_dev, dtype=jnp.int32)).astype(jnp.float32)
    col_ids = (tile_me * cols_dev + jnp.arange(cols_dev, dtype=jnp.int32)).astype(jnp.float32)
    vcoord = row_ids + 0.5 - total_rows / 2.0
    ucoord = col_ids + 0.5 - total_cols / 2.0
    weight = dist / jnp.sqrt(dist * dist + ucoord[None, :] ** 2 + vcoord[:, None] ** 2)
    weighted = (raw.astype(jnp.float32) * weight[None]).astype(jnp.bfloat16)
    padded = with_halo(weighted, (("tile", 2),), 128)
    tiles = tap_tiles()
    blocks = cols_dev // 128
    total = jnp.zeros((proj_count, rows_dev, blocks, 128), jnp.float32)
    for index in range(3):
        piece = padded[:, :, 128 * index : 128 * index + cols_dev].reshape(
            proj_count, rows_dev, blocks, 128
        )
        total = total + jnp.einsum(
            "prna,ab->prnb", piece, tiles[index], preferred_element_type=jnp.float32
        )
    filtered = total.reshape(proj_count, rows_dev, cols_dev).astype(jnp.bfloat16)
    owned = lax.all_to_all(filtered, "proj", split_axis=0, concat_axis=1, tiled=True)
    local_count = owned.shape[0]
    first_proj = proj_me * local_count
    starts = lax.dynamic_slice_in_dim(band_start, first_proj, local_count, 0)
    lengths = lax.dynamic_slice_in_dim(band_length, first_proj, local_count, 0)
    win_cols = col_weights.shape[2]
    my_offsets = col_offset[:, 0]

    def cut_window(band_rows, offset):
        return lax.dynamic_slice_in_dim(band_rows, offset * 128, win_cols, 1)

    full = lax.all_gather(owned, "tile", axis=2, tiled=True)
    my_starts = lax.dynamic_slice_in_dim(starts, tile_me, 1, 1)[:, 0]
    my_lengths = lax.dynamic_slice_in_dim(lengths, tile_me, 1, 1)[:, 0]
    bands = jax.vmap(take_band)(full, my_starts, my_lengths)
    windows = jax.vmap(cut_window)(bands, my_offsets)
    acc = jnp.zeros((row_weights.shape[2], col_weights.shape[3]), jnp.float32)
    for local in range(local_count):
        spread = jnp.dot(
            windows[local], col_weights[local, 0], preferred_element_type=jnp.float32
        ).astype(jnp.bfloat16)
        acc = acc + jnp.dot(row_weights[local, 0], spread, preferred_element_type=jnp.float32)
    return lax.psum_scatter(acc, "proj", scatter_dimension=0, tiled=True)


def solution(mesh):
    return jax.shard_map(
        body,
        mesh=mesh,
        in_specs=(
            P(None, "proj", "tile"),
            P("proj", "tile", None, None),
            P("proj", "tile", None, None),
            P(),
            P(),
            P("proj", "tile"),
        ),
        out_specs=P("proj", "tile"),
        check_vma=False,
    )
```

profile of v0, /device:TPU:16, one launch (start us, length us, event | category | flops | bytes accessed | tf_op | source)
XLA Modules:
  0.0 398.0 jit_solution(17064370836072021085)
XLA Ops:
  6.5 0.0 copy-start
  6.5 0.0 copy-start.1
  6.5 0.0 all-gather.2.cloned.1.call-start
  6.6 0.1 rsqrt_multiply_fusion
  6.7 1.6 multiply_convert_fusion
  8.2 0.3 fusion.134
  8.5 3.6 collective-permute-start
  12.1 3.8 collective-permute-start.1
  15.9 0.0 copy-done.1
  15.9 0.5 fusion.21
  16.4 20.4 %collective-permute-done = bf16[32,64,128]{2,1,0:T(8,128)(2,1)S(1)} collective-permute-done((bf16[32,64,128]{2,1,0:T(8,128)(2,1)S(1)}, bf16[32,64,128]{2,1,0:T(8,128)(2,1)S(1)}, u32[]{:S(2)}, u32[]{:S(2)}) %collective-permute-start) | collective-permute-done | bytes 524320 | tf_op jit(solution)/shard_map/ppermute | solution.py:17
  36.8 0.0 collective-permute-done.1
  36.8 0.4 fusion.27
  37.2 0.4 fusion.24
  37.7 0.5 fusion.16
  38.2 0.0 copy-start.3
  38.2 0.2 copy.57
  38.4 21.4 %all_to_all.18 = bf16[32,64,256]{2,1,0:T(8,128)(2,1)S(1)} all-to-all(bf16[32,64,256]{2,1,0:T(8,128)(2,1)S(1)} %bitcast.91), channel_id=1, replica_groups=mesh['proj'=16,'tile'=16] {'proj'}, dimensions={0} | all-to-all | bytes 2097152 | tf_op jit(solution)/shard_map/all_to_all | solution.py:76
  59.8 1.0 copy.30
  60.9 0.0 all-gather.2.cloned.1.call-update
  60.9 0.0 reduce-scatter.4.cloned.1.call-start
  61.0 0.8 dynamic_slice.12
  61.7 0.1 copy.39
  61.8 0.0 copy-done.3
  61.8 0.1 copy.32
  61.9 0.0 copy-done
  61.9 0.1 dynamic-slice_bitcast_fusion
  62.0 0.1 pad_add_fusion
  62.1 0.1 iota_compare_fusion
  62.2 235.7 %all-gather.2.cloned.1.call-done = bf16[2,1024,4096]{2,1,0:T(8,128)(2,1)} async-done(((bf16[2,1024,256]{2,1,0:T(8,128)(2,1)}), bf16[2,1024,4096]{2,1,0:T(8,128)(2,1)}) %all-gather.2.cloned.1.call-update) | async-done | bytes 16777232 | tf_op jit(solution)/shard_map/all_gather | solution.py:87
  297.8 10.6 %while.4 = (s32[]{:T(128)}, bf16[2,1024,4096]{2,1,0:T(8,128)(2,1)}, s32[2,3]{1,0:T(2,128)S(1)}, bf16[2,256,4096]{2,1,0:T(8,128)(2,1)}) while((s32[]{:T(128)}, bf16[2,1024,4096]{2,1,0:T(8,128)(2,1)}, s32[2,3]{1,0:T(2,128)S(1)}, bf16[2,256,4096]{2,1,0:T(8,128)(2,1)}) %tuple.45), condition=%wide.while_cond.clone, body=%wide.while_body.sunk.clone | while | flops 2 | bytes 4195937 | solution.py:46
  297.8 0.6 fusion.142
  298.4 4.7 %dynamic-slice_dynamic-update-slice_fusion.6 = bf16[2,256,4096]{2,1,0:T(8,128)(2,1)} fusion(bf16[2,256,4096]{2,1,0:T(8,128)(2,1)} %get-tuple-element.138, s32[]{:T(128)} %get-tuple-element.135, bf16[2,1024,4096]{2,1,0:T(8,128)(2,1)} %get-tuple-element.140, s32[]{:T(128)} %bitcast.86, s32[]{:T(128)} %bitcast.87), kind=kLoop, calls=%fused_computation.clone.1.clone | loop fusion | bytes 4195840 | tf_op jit(solution)/shard_map/vmap()/gather
  303.1 0.6 fusion.142
  303.7 4.7 %dynamic-slice_dynamic-update-slice_fusion.6 = bf16[2,256,4096]{2,1,0:T(8,128)(2,1)} fusion(bf16[2,256,4096]{2,1,0:T(8,128)(2,1)} %get-tuple-element.138, s32[]{:T(128)} %get-tuple-element.135, bf16[2,1024,4096]{2,1,0:T(8,128)(2,1)} %get-tuple-element.140, s32[]{:T(128)} %bitcast.86, s32[]{:T(128)} %bitcast.87), kind=kLoop, calls=%fused_computation.clone.1.clone | loop fusion | bytes 4195840 | tf_op jit(solution)/shard_map/vmap()/gather
  308.4 4.5 %broadcast_select_fusion = bf16[2,256,4096]{2,1,0:T(8,128)(2,1)} fusion(bf16[2,256,4096]{2,1,0:T(8,128)(2,1)} %get-tuple-element.12, pred[2,256]{1,0:T(4,128)(4,1)S(1)} %iota_compare_fusion), kind=kLoop, calls=%fused_computation.10 | loop fusion | flops 2097152 | bytes 8389120 | tf_op jit(solution)/shard_map/vmap(jit(_where))/select_n | solution.py:42
  312.9 0.0 copy-start.2
  312.9 6.4 %while.5 = (s32[]{:T(128)}, bf16[2,256,4096]{2,1,0:T(8,128)(2,1)}, s32[2,3]{1,0:T(2,128)S(1)}, bf16[2,256,1024]{2,1,0:T(8,128)(2,1)S(1)}) while((s32[]{:T(128)}, bf16[2,256,4096]{2,1,0:T(8,128)(2,1)}, s32[2,3]{1,0:T(2,128)S(1)}, bf16[2,256,1024]{2,1,0:T(8,128)(2,1)S(1)}) %tuple.48), condition=%wide.while_cond.1.clone, body=%wide.while_body.1.sunk.clone | while | flops 2 | bytes 1048685 | solution.py:85
  312.9 0.6 fusion.143
  313.6 2.5 dynamic-slice_dynamic-update-slice_fusion.7
  316.1 0.6 fusion.143
  316.8 2.5 dynamic-slice_dynamic-update-slice_fusion.7
  319.3 0.0 copy-done.2
  319.3 3.8 fusion.14
  323.1 3.8 fusion.12
  326.9 1.3 copy.37
  328.2 0.0 reduce-scatter.4.cloned.1.call-update
  328.2 63.0 %reduce-scatter.4.cloned.1.call-done = f32[8,2048]{1,0:T(8,128)} async-done(((f32[128,2048]{1,0:T(8,128)}), f32[8,2048]{1,0:T(8,128)}) %reduce-scatter.4.cloned.1.call-update) | async-done | bytes 65552 | tf_op jit(solution)/shard_map/reduce_scatter | solution.py:98
  (10 shorter events, 0.0 us)
Async XLA Ops:
  6.5 55.4 %copy-start = (s32[32,16]{0,1:T(8,128)S(1)}, s32[32,16]{0,1:T(8,128)}, u32[]{:S(2)}) copy-start(s32[32,16]{0,1:T(8,128)} %param.10) | copy-start | bytes 6148
  6.5 9.4 %copy-start.1 = (bf16[32,64,256]{2,1,0:T(8,128)(2,1)S(1)}, bf16[32,64,256]{2,1,0:T(8,128)(2,1)}, u32[]{:S(2)}) copy-start(bf16[32,64,256]{2,1,0:T(8,128)(2,1)} %param.6) | copy-start | bytes 3145732
  6.5 291.3 %all-gather.2.cloned.1.call-start = ((), (), s32[]{:S(2)}) async-start(), calls=%async_computation.2 | async-start | bytes 17825792 | tf_op jit(solution)/shard_map/all_gather | solution.py:87
  8.5 28.3 %collective-permute-start = (bf16[32,64,128]{2,1,0:T(8,128)(2,1)S(1)}, bf16[32,64,128]{2,1,0:T(8,128)(2,1)S(1)}, u32[]{:S(2)}, u32[]{:S(2)}) collective-permute-start(bf16[32,64,128]{2,1,0:T(8,128)(2,1)S(1)} %get-tuple-element.44), channel_id=1, source_target_pairs={{0,1},{1,2},{2,3},{3,4},{4,5},{5,6},{6,7},{7,8},{8,9},{9,10},{10,1... | collective-permute-start | bytes 1572872 | tf_op jit(solution)/shard_map/ppermute | solution.py:17
  12.1 24.7 %collective-permute-start.1 = (bf16[32,64,128]{2,1,0:T(8,128)(2,1)S(1)}, bf16[32,64,128]{2,1,0:T(8,128)(2,1)S(1)}, u32[]{:S(2)}, u32[]{:S(2)}) collective-permute-start(bf16[32,64,128]{2,1,0:T(8,128)(2,1)S(1)} %get-tuple-element.43), channel_id=1, source_target_pairs={{1,0},{2,1},{3,2},{4,3},{5,4},{6,5},{7,6},{8,7},{9,8},{10,9},{11,1... | collective-permute-start | bytes 1572872 | tf_op jit(solution)/shard_map/ppermute | solution.py:18
  38.2 23.6 %copy-start.3 = (s32[2,1]{0,1:T(1,128)S(1)}, s32[2,1]{0,1:T(1,128)}, u32[]{:S(2)}) copy-start(s32[2,1]{0,1:T(1,128)} %param.11) | copy-start | bytes 28
  60.9 330.3 %reduce-scatter.4.cloned.1.call-start = ((), (), s32[]{:S(2)}) async-start(), calls=%async_computation.3 | async-start | bytes 1114112 | tf_op jit(solution)/shard_map/reduce_scatter | solution.py:98
  312.9 6.4 %copy-start.2 = (bf16[2,1,128,256]{3,2,1,0:T(8,128)(2,1)S(1)}, bf16[2,1,128,256]{3,2,1,0:T(8,128)(2,1)}, u32[]{:S(2)}) copy-start(bf16[2,1,128,256]{3,2,1,0:T(8,128)(2,1)} %param.7) | copy-start | bytes 393220
Sparse Core Ops, SparseCore 0:
  61.0 236.7 all-gather.1
  328.4 62.7 reduce-scatter.3
where the time goes:
time: 399 us; the launch traced here: 398 us
  waiting for transfers between devices  319 us (80%)
  blocking collectives  21.4 us (5%)
  local copies, waits for them, and re-layouts  20.8 us (5%)
  between operations  13.6 us (3%)
  matrix products  9.01 us (2%)
  starting transfers between devices  7.42 us (2%)
  other arithmetic  6.68 us (2%)
    all_gather x1, waiting for transfers between devices, body(): full = lax.all_gather(owned, 'tile', axis=2, tiled=True)  236 us
    reduce_scatter x1, waiting for transfers between devices, body(): return lax.psum_scatter(acc, 'proj', scatter_dimension=0, tiled=True)  63 us
    all_to_all x1, blocking collectives, body(): lax.all_to_all(filtered, 'proj', split_axis=0, concat_axis=1, tiled=True)  21.4 us
    ppermute x1, waiting for transfers between devices, with_halo(): before = lax.ppermute(last, axis, up)  20.4 us
    gather x12, local copies, waits for them, and re-layouts  16.9 us
  transfers between devices with their start and end apart: 4, of which 3 were waited for; matrix products, arithmetic and copies ran while one was open for 0% of the time, Pallas kernels for 0%

commit v1 on v0

--- a/solution.py
+++ b/solution.py
@@ -84,7 +84,8 @@
     def cut_window(band_rows, offset):
         return lax.dynamic_slice_in_dim(band_rows, offset * 128, win_cols, 1)
 
-    full = lax.all_gather(owned, "tile", axis=2, tiled=True)
+    stack = jnp.stack([owned] * lax.axis_size("tile"))
+    full = jnp.concatenate(lax.all_to_all(stack, "tile", 0, 0), axis=2)
     my_starts = lax.dynamic_slice_in_dim(starts, tile_me, 1, 1)[:, 0]
     my_lengths = lax.dynamic_slice_in_dim(lengths, tile_me, 1, 1)[:, 0]
     bands = jax.vmap(take_band)(full, my_starts, my_lengths)

time: 399 us -> 594 us (1.49)
  waiting for transfers between devices: 319 us -> 462 us
  local copies, waits for them, and re-layouts: 20.8 us -> 58.8 us
  starting transfers between devices: 7.42 us -> 19.9 us
    all_to_all x0 -> x1, waiting for transfers between devices: none -> 381 us  [body(): full = jnp.concatenate(lax.all_to_all(stack, 'tile', 0, 0), axis=2)]
    all_gather x1 -> x0, waiting for transfers between devices: 236 us -> none  [body(): full = lax.all_gather(owned, 'tile', axis=2, tiled=True)]
    all_to_all x0 -> x1, local copies, waits for them, and re-layouts: none -> 22.4 us  [body(): full = jnp.concatenate(lax.all_to_all(stack, 'tile', 0, 0), axis=2)]
    all_to_all x0 -> x1, starting transfers between devices: none -> 11.6 us  [body(): full = jnp.concatenate(lax.all_to_all(stack, 'tile', 0, 0), axis=2)]
    gather x12 -> x16, local copies, waits for them, and re-layouts: 16.9 us -> 27.4 us
    ppermute x1, waiting for transfers between devices: 0.01 us -> 9.31 us  [with_halo(): after = lax.ppermute(leading, axis, down)]
    ppermute x1, waiting for transfers between devices: 20.4 us -> 11.1 us  [with_halo(): before = lax.ppermute(last, axis, up)]
    another operation x0 -> x1, local copies, waits for them, and re-layouts: none -> 5.94 us  [body(): stack = jnp.stack([owned] * lax.axis_size('tile'))]
  transfers between devices with their start and end apart: 4 -> 4, of which waited for: 3 -> 4; matrix products, arithmetic and copies ran while one was open for 0% -> 0% of each run, Pallas kernels for 0% -> 0%
where the time goes in v1:
time: 594 us; the launch traced here: 593 us
  waiting for transfers between devices  462 us (78%)
  local copies, waits for them, and re-layouts  58.8 us (10%)
  blocking collectives  21.4 us (4%)
  starting transfers between devices  19.9 us (3%)
  between operations  13.5 us (2%)
  matrix products  10.3 us (2%)
  other arithmetic  6.7 us (1%)
    all_to_all x1, waiting for transfers between devices, body(): full = jnp.concatenate(lax.all_to_all(stack, 'tile', 0, 0), axis=2)  381 us
    reduce_scatter x1, waiting for transfers between devices, body(): return lax.psum_scatter(acc, 'proj', scatter_dimension=0, tiled=True)  60.8 us
    gather x16, local copies, waits for them, and re-layouts  27.4 us
    all_to_all x1, local copies, waits for them, and re-layouts, body(): full = jnp.concatenate(lax.all_to_all(stack, 'tile', 0, 0), axis=2)  22.4 us
    all_to_all x1, blocking collectives, body(): lax.all_to_all(filtered, 'proj', split_axis=0, concat_axis=1, tiled=True)  21.4 us
  transfers between devices with their start and end apart: 4, of which 4 were waited for; matrix products, arithmetic and copies ran while one was open for 0% of the time, Pallas kernels for 0%

profile of v1, /device:TPU:16, one launch (start us, length us, event | category | flops | bytes accessed | tf_op | source)
XLA Modules:
  0.0 592.7 jit_solution(11277636174936657185)
XLA Ops:
  6.5 0.0 copy-start
  6.6 0.1 rsqrt_multiply_fusion
  6.6 0.0 copy-start.2
  6.7 1.6 multiply_convert_fusion
  8.2 0.3 fusion.134
  8.5 4.0 collective-permute-start.1
  12.5 4.3 collective-permute-start
  16.8 0.0 copy-done.2
  16.8 0.5 fusion.21
  17.3 9.3 %collective-permute-done.1 = bf16[32,64,128]{2,1,0:T(8,128)(2,1)S(1)} collective-permute-done((bf16[32,64,128]{2,1,0:T(8,128)(2,1)S(1)}, bf16[32,64,128]{2,1,0:T(8,128)(2,1)S(1)}, u32[]{:S(2)}, u32[]{:S(2)}) %collective-permute-start.1) | collective-permute-done | bytes 524320 | tf_op jit(solution)/shard_map/ppermute | solution.py:18
  26.6 11.1 %collective-permute-done = bf16[32,64,128]{2,1,0:T(8,128)(2,1)S(1)} collective-permute-done((bf16[32,64,128]{2,1,0:T(8,128)(2,1)S(1)}, bf16[32,64,128]{2,1,0:T(8,128)(2,1)S(1)}, u32[]{:S(2)}, u32[]{:S(2)}) %collective-permute-start) | collective-permute-done | bytes 524320 | tf_op jit(solution)/shard_map/ppermute | solution.py:17
  37.7 0.4 fusion.27
  38.1 0.5 fusion.24
  38.6 0.5 fusion.16
  39.1 0.2 copy.68
  39.3 21.4 %all_to_all.20 = bf16[32,64,256]{2,1,0:T(8,128)(2,1)S(1)} all-to-all(bf16[32,64,256]{2,1,0:T(8,128)(2,1)S(1)} %bitcast.95), channel_id=1, replica_groups=mesh['proj'=16,'tile'=16] {'proj'}, dimensions={0} | all-to-all | bytes 2097152 | tf_op jit(solution)/shard_map/all_to_all | solution.py:76
  60.7 0.1 copy.38
  60.8 5.9 %stack.5 = bf16[16,2,1024,256]{3,2,1,0:T(8,128)(2,1)} broadcast(bf16[2,1024,256]{2,1,0:T(8,128)(2,1)S(1)} %bitcast.94), dimensions={1,2,3} | broadcast | bytes 17825792 | tf_op jit(solution)/shard_map/stack | solution.py:87
  66.7 0.0 copy-start.4
  66.7 11.6 %all-to-all-start.1 = ((bf16[16,2,1024,256]{3,2,1,0:T(8,128)(2,1)}), bf16[16,2,1024,256]{3,2,1,0:T(8,128)(2,1)}, u32[]{:S(2)}, u32[]{:S(2)}) async-start(bf16[16,2,1024,256]{3,2,1,0:T(8,128)(2,1)} %stack.5), calls=%async_computation.1 | async-start | bytes 33554432 | tf_op jit(solution)/shard_map/all_to_all | solution.py:88
  78.3 0.0 reduce-scatter.4.cloned.1.call-start
  78.4 0.0 copy-done.4
  78.4 0.1 copy.42
  78.5 0.8 dynamic_slice.12
  79.3 0.1 copy.50
  79.4 0.0 copy-done
  79.4 0.1 dynamic-slice_bitcast_fusion
  79.4 0.1 pad_add_fusion
  79.5 0.1 iota_compare_fusion
  79.6 380.9 %all-to-all-done.1 = bf16[16,2,1024,256]{3,2,1,0:T(8,128)(2,1)} async-done(((bf16[16,2,1024,256]{3,2,1,0:T(8,128)(2,1)}), bf16[16,2,1024,256]{3,2,1,0:T(8,128)(2,1)}, u32[]{:S(2)}, u32[]{:S(2)}) %all-to-all-start.1) | async-done | bytes 16777248 | tf_op jit(solution)/shard_map/all_to_all | solution.py:88
  460.5 22.4 %copy.39 = bf16[16,2,1024,256]{2,3,0,1:T(8,128)(2,1)} copy(bf16[16,2,1024,256]{3,2,1,0:T(8,128)(2,1)} %all-to-all-done.1) | data formatting | bytes 33554432 | tf_op jit(solution)/shard_map/all_to_all | solution.py:88
  482.9 21.1 %while.4 = (s32[]{:T(128)}, bf16[2,1024,4096]{1,2,0:T(8,128)(2,1)}, s32[2,3]{1,0:T(2,128)S(1)}, bf16[2,256,4096]{2,1,0:T(8,128)(2,1)}) while((s32[]{:T(128)}, bf16[2,1024,4096]{1,2,0:T(8,128)(2,1)}, s32[2,3]{1,0:T(2,128)S(1)}, bf16[2,256,4096]{2,1,0:T(8,128)(2,1)}) %tuple.54), condition=%wide.while_cond.clone, body=%wide.while_body.sunk.clone | while | flops 2 | bytes 12583029 | solution.py:46
  482.9 0.6 fusion.142
  483.5 5.5 constant_dynamic-slice_fusion.10
  489.1 2.9 copy.71
  492.0 1.4 constant_dynamic-update-slice_fusion.3
  493.4 0.6 fusion.142
  494.0 5.5 constant_dynamic-slice_fusion.10
  499.6 2.9 copy.71
  502.5 1.5 constant_dynamic-update-slice_fusion.3
  504.0 4.5 broadcast_select_fusion
  508.5 0.0 copy-start.3
  508.5 6.4 %while.5 = (s32[]{:T(128)}, bf16[2,256,4096]{2,1,0:T(8,128)(2,1)}, s32[2,3]{1,0:T(2,128)S(1)}, bf16[2,256,1024]{2,1,0:T(8,128)(2,1)S(1)}) while((s32[]{:T(128)}, bf16[2,256,4096]{2,1,0:T(8,128)(2,1)}, s32[2,3]{1,0:T(2,128)S(1)}, bf16[2,256,1024]{2,1,0:T(8,128)(2,1)S(1)}) %tuple.49), condition=%wide.while_cond.1.clone, body=%wide.while_body.1.sunk.clone | while | flops 2 | bytes 1048693 | solution.py:85
  508.5 0.6 fusion.143
  509.2 2.5 dynamic-slice_dynamic-update-slice_fusion.3
  511.7 0.6 fusion.143
  512.4 2.5 dynamic-slice_dynamic-update-slice_fusion.3
  514.9 0.0 copy-done.3
  514.9 4.7 fusion.14
  519.7 0.0 copy-start.1
  519.7 4.1 fusion.12
  523.7 1.3 copy.47
  525.1 0.0 reduce-scatter.4.cloned.1.call-update
  525.1 60.8 %reduce-scatter.4.cloned.1.call-done = f32[8,2048]{1,0:T(8,128)} async-done(((f32[128,2048]{1,0:T(8,128)}), f32[8,2048]{1,0:T(8,128)}) %reduce-scatter.4.cloned.1.call-update) | async-done | bytes 65552 | tf_op jit(solution)/shard_map/reduce_scatter | solution.py:99
  585.9 0.0 copy-done.1
  (10 shorter events, 0.0 us)
Async XLA Ops:
  6.5 72.8 %copy-start = (s32[32,16]{0,1:T(8,128)S(1)}, s32[32,16]{0,1:T(8,128)}, u32[]{:S(2)}) copy-start(s32[32,16]{0,1:T(8,128)} %param.10) | copy-start | bytes 6148
  6.6 10.2 %copy-start.2 = (bf16[32,64,256]{2,1,0:T(8,128)(2,1)S(1)}, bf16[32,64,256]{2,1,0:T(8,128)(2,1)}, u32[]{:S(2)}) copy-start(bf16[32,64,256]{2,1,0:T(8,128)(2,1)} %param.6) | copy-start | bytes 3145732
  8.5 18.1 %collective-permute-start.1 = (bf16[32,64,128]{2,1,0:T(8,128)(2,1)S(1)}, bf16[32,64,128]{2,1,0:T(8,128)(2,1)S(1)}, u32[]{:S(2)}, u32[]{:S(2)}) collective-permute-start(bf16[32,64,128]{2,1,0:T(8,128)(2,1)S(1)} %get-tuple-element.47), channel_id=1, source_target_pairs={{1,0},{2,1},{3,2},{4,3},{5,4},{6,5},{7,6},{8,7},{9,8},{10,9},{11,1... | collective-permute-start | bytes 1572872 | tf_op jit(solution)/shard_map/ppermute | solution.py:18
  12.5 25.2 %collective-permute-start = (bf16[32,64,128]{2,1,0:T(8,128)(2,1)S(1)}, bf16[32,64,128]{2,1,0:T(8,128)(2,1)S(1)}, u32[]{:S(2)}, u32[]{:S(2)}) collective-permute-start(bf16[32,64,128]{2,1,0:T(8,128)(2,1)S(1)} %get-tuple-element.48), channel_id=1, source_target_pairs={{0,1},{1,2},{2,3},{3,4},{4,5},{5,6},{6,7},{7,8},{8,9},{9,10},{10,1... | collective-permute-start | bytes 1572872 | tf_op jit(solution)/shard_map/ppermute | solution.py:17
  66.7 11.7 %copy-start.4 = (s32[2,1]{0,1:T(1,128)S(1)}, s32[2,1]{0,1:T(1,128)}, u32[]{:S(2)}) copy-start(s32[2,1]{0,1:T(1,128)} %param.11) | copy-start | bytes 28
  66.7 393.7 %all-to-all-start.1 = ((bf16[16,2,1024,256]{3,2,1,0:T(8,128)(2,1)}), bf16[16,2,1024,256]{3,2,1,0:T(8,128)(2,1)}, u32[]{:S(2)}, u32[]{:S(2)}) async-start(bf16[16,2,1024,256]{3,2,1,0:T(8,128)(2,1)} %stack.5), calls=%async_computation.1 | async-start | bytes 33554432 | tf_op jit(solution)/shard_map/all_to_all | solution.py:88
  78.3 507.6 %reduce-scatter.4.cloned.1.call-start = ((), (), s32[]{:S(2)}) async-start(), calls=%async_computation.3 | async-start | bytes 1114112 | tf_op jit(solution)/shard_map/reduce_scatter | solution.py:99
  508.5 6.4 %copy-start.3 = (bf16[2,1,128,256]{3,2,1,0:T(8,128)(2,1)S(1)}, bf16[2,1,128,256]{3,2,1,0:T(8,128)(2,1)}, u32[]{:S(2)}) copy-start(bf16[2,1,128,256]{3,2,1,0:T(8,128)(2,1)} %param.7) | copy-start | bytes 393220
  519.7 66.2 %copy-start.1 = (s32[32,16]{0,1:T(8,128)S(1)}, s32[32,16]{0,1:T(8,128)}, u32[]{:S(2)}) copy-start(s32[32,16]{0,1:T(8,128)} %param.10) | copy-start | bytes 6148
Sparse Core Ops, SparseCore 0:
  525.2 60.6 reduce-scatter.3
